TPU v7x, 512 devices: a whole 4x4x16 slice. The times are simulated.
512 devices in a mesh: img: 16 (over x, z_hi), band: 32 (over y, z_lo, core).
Axes of the slice: x: 4, y: 4, z: 16 (z_hi: 4, z_lo: 4; z = z_hi * 4 + z_lo), core: 2. Of those that a mesh axis runs over, the one named last changes fastest.
Arguments:
- latents: bfloat16 [16, 64, 64, 1120], P('img', 'band'), may hold values from -6 to 6
- tangents: bfloat16 [16, 64, 64, 1120], P('img', 'band'), may hold values from -6 to 6
- w_expand: bfloat16 [1120, 5632], P('img', 'band'), may hold values from -0.1875 to 0.1875
- b_expand: bfloat16 [5632], P('band'), may hold values from -3 to 3
- w_depth: bfloat16 [9, 5632], P(None, 'band'), may hold values from -2 to 2
- b_depth: bfloat16 [5632], P('band'), may hold values from -3 to 3
Outputs:
- gated: bfloat16 [16, 64, 64, 2816], P('img', 'band')
- gated_tangent: bfloat16 [16, 64, 64, 2816], P('img', 'band')
All inputs are finite; a program needn't handle non-finite values.
Results may differ from a plain program's by a relative error of at most 0.0057.
Values may be sent and summed in bfloat16 or wider, within the bound.
No kernel may reach another device: no remote copies, remote signals or barrier semaphores. Data moves between devices by JAX's collectives and lax.ppermute only.
A program may use at most 64 MiB of HBM per device.

v0:
```python
import jax
import jax.numpy as jnp
from jax import lax
from jax.sharding import PartitionSpec as P


def extended(cells, sides, width):
    for axis, dim in sides:
        count = lax.axis_size(axis)
        ends = count - 1
        head = lax.slice_in_dim(cells, 0, width, axis=dim)
        tail = lax.slice_in_dim(cells, cells.shape[dim] - width, cells.shape[dim], axis=dim)
        cells = jnp.concatenate(
            [
                lax.ppermute(tail, axis, [(i, (i + 1) % count) for i in range(ends)]),
                cells,
                lax.ppermute(head, axis, [((i + 1) % count, i) for i in range(ends)]),
            ],
            axis=dim,
        )
    return cells


def tangent_act(primal_pre, tangent_pre):
    sigmoid_v = jax.nn.sigmoid(primal_pre)
    value = primal_pre * sigmoid_v
    slope = sigmoid_v * (1.0 + primal_pre * (1.0 - sigmoid_v))
    return (value, slope * tangent_pre)


def depthwise(padded, depth_taps, row_count, col_count):
    total = jnp.zeros(padded.shape[:-3] + (row_count, col_count, padded.shape[-1]), jnp.float32)
    for row_off in range(3):
        for col_off in range(3):
            window = padded[
                ..., row_off : row_off + row_count, col_off : col_off + col_count, :
            ].astype(jnp.float32)
            total = total + window * depth_taps[3 * row_off + col_off].astype(jnp.float32)
    return total


def finish(mixed, depth_bias, half):
    primal_mix = mixed[0] + depth_bias.astype(jnp.float32)
    tangent_mix = mixed[1]
    gate_value, gate_tangent = tangent_act(primal_mix[..., half:], tangent_mix[..., half:])
    gated = primal_mix[..., :half] * gate_value
    gated_tangent = tangent_mix[..., :half] * gate_value + primal_mix[..., :half] * gate_tangent
    return (gated.astype(jnp.bfloat16), gated_tangent.astype(jnp.bfloat16))


def activate(pre_act, expand_bias, token_count):
    bias_cols = expand_bias.astype(jnp.float32)
    value, slope_tangent = tangent_act(pre_act[:token_count] + bias_cols, pre_act[token_count:])
    return jnp.concatenate([value.astype(jnp.bfloat16), slope_tangent.astype(jnp.bfloat16)], 0)


def on_device(latents, tangents, w_expand, b_expand, w_depth, b_depth):
    image_count, row_count, col_count, channels = latents.shape
    depth_taps, expand_bias, depth_bias = (
        lax.all_gather(w_depth, "band", axis=1, tiled=True),
        lax.all_gather(b_expand, "band", axis=0, tiled=True),
        lax.all_gather(b_depth, "band", axis=0, tiled=True),
    )
    full_width = expand_bias.shape[0]
    half = full_width // 2
    both_inputs = jnp.stack([latents, tangents])
    span_rows = both_inputs.shape[2]
    token_count = image_count * span_rows * col_count
    stacked = both_inputs.reshape(2 * token_count, channels)
    weight_rows = lax.all_gather(w_expand, "img", axis=0, tiled=True)
    pre_act = jnp.dot(
        stacked,
        lax.all_gather(weight_rows, "band", axis=1, tiled=True),
        preferred_element_type=jnp.float32,
    )
    activated = activate(pre_act, expand_bias, token_count)
    activated = activated.reshape(2, image_count, span_rows, col_count, full_width)
    padded = extended(activated, (("band", 2),), 1)
    padded = jnp.pad(padded, ((0, 0), (0, 0), (0, 0), (1, 1), (0, 0)))
    mixed = depthwise(padded, depth_taps, row_count, col_count)
    return finish(mixed, depth_bias, half)


def solution(mesh):
    placed = (
        P("img", "band", None, None),
        P("img", "band", None, None),
        P("img", "band"),
        P("band"),
        P(None, "band"),
        P("band"),
    )
    return jax.shard_map(
        on_device,
        mesh=mesh,
        in_specs=placed,
        out_specs=(P("img", "band", None, None), P("img", "band", None, None)),
        check_vma=False,
    )
```

profile of v0, /device:TPU:33, one launch (start us, length us, event | category | flops | bytes accessed | tf_op | source)
XLA Modules:
  0.0 304.1 jit_solution(5817018077975962852)
XLA Ops:
  7.2 0.0 all-gather.4.cloned.1.call-start
  7.3 57.8 %all-gather = bf16[16,70,176]{2,1,0:T(8,128)(2,1)S(1)} all-gather(bf16[1,70,176]{2,1,0:T(8,128)(2,1)} %bitcast.34), channel_id=1, replica_groups=mesh['img'=16,'band'=32] {'img'}, dimensions={0}, use_global_device_ids=true | all-gather | bytes 418880 | tf_op jit(solution)/shard_map/all_gather | solution.py:70
  65.1 0.2 reshape.144
  65.3 1.0 copy.30
  66.3 1.3 dynamic-slice
  68.2 0.2 dynamic-update-slice
  68.5 0.2 dynamic-update-slice.1
  68.7 134.4 %all-reduce.3 = (bf16[5632]{0:T(1024)(128)(2,1)S(1)}, bf16[5632]{0:T(1024)(128)(2,1)S(1)}) all-reduce(bf16[5632]{0:T(1024)(128)(2,1)S(1)} %dynamic-update-slice, bf16[5632]{0:T(1024)(128)(2,1)S(1)} %dynamic-update-slice.1), channel_id=1, replica_groups=mesh['img'=16,'band'=32] {'band'}, use_global_device_ids=true, to_apply=%add.1 | all-reduce | flops 11264 | bytes 45056
  203.2 0.1 pad_maximum_fusion.3
  203.3 7.0 %fusion.22 = f32[256,5632]{1,0:T(8,128)S(1)} fusion(bf16[256,1120]{1,0:T(8,128)(2,1)S(1)} %bitcast.31, bf16[1120,5632]{0,1:T(8,128)(2,1)} %all-gather.4.cloned.1.call-done), kind=kOutput, calls=%fused_computation.48 | convolution fusion | flops 3229614080 | bytes 18956288 | tf_op jit(solution)/shard_map/dot_general | solution.py:71
  210.4 1.4 multiply_convert_fusion
  211.7 0.2 pad_maximum_fusion.2
  211.9 1.8 fusion.21
  213.7 8.1 %collective-permute-start.1 = (bf16[2,1,1,64,5632]{4,3,2,1,0:T(8,128)(2,1)}, bf16[2,1,1,64,5632]{4,3,2,1,0:T(8,128)(2,1)}, u32[]{:S(2)}, u32[]{:S(2)}) collective-permute-start(bf16[2,1,1,64,5632]{4,3,2,1,0:T(8,128)(2,1)} %get-tuple-element.18), channel_id=1, source_target_pairs={{1,0},{2,1},{3,2},{4,3},{5,4},{6,5},{7,6},{8,7},{9,8},{10,9},{11,1... | collective-permute-start | bytes 4325384 | tf_op jit(solution)/shard_map/ppermute | solution.py:17
  221.8 1.9 collective-permute-start
  223.7 59.7 %all-gather.1 = bf16[32,176,9]{1,2,0:T(8,128)(2,1)S(1)} all-gather(bf16[1,176,9]{1,2,0:T(8,128)(2,1)S(1)} %bitcast.35), channel_id=1, replica_groups=mesh['img'=16,'band'=32] {'band'}, dimensions={0}, use_global_device_ids=true | all-gather | bytes 104544 | tf_op jit(solution)/shard_map/all_gather | solution.py:60
  283.4 0.1 copy.26
  283.4 0.3 reshape.139
  283.7 0.6 fusion.20
  284.3 3.8 %fusion.5 = bf16[2,1,4,66,5632]{4,3,2,1,0:T(8,128)(2,1)S(1)} fusion(bf16[2,1,1,64,5632]{4,3,2,1,0:T(8,128)(2,1)} %collective-permute-done.1, bf16[2,1,2,64,5632]{4,3,2,1,0:T(8,128)(2,1)S(1)} %bitcast.28, bf16[2,1,1,64,5632]{4,3,2,1,0:T(8,128)(2,1)} %collective-permute-done), kind=kLoop, calls=%fused_computation.7 | loop fusion | flops 35684352 | bytes 11714560 | tf_op jit(solution)/shard_map/concatenate | solution.py:13
  288.2 6.8 %multiply_add_fusion = f32[2,1,2,64,5632]{4,3,2,1,0:T(8,128)S(1)} fusion(bf16[2,1,2,64,5632]{4,3,2,1,0:T(8,128)(2,1)S(1)} %bitcast.29, bf16[2,1,4,66,5632]{4,3,2,1,0:T(8,128)(2,1)S(1)} %fusion.5, bf16[2,1,1,64,5632]{4,3,2,1,0:T(8,128)(2,1)} %collective-permute-done.1, bf16[2,1,1,64,5632]{4,3,2,1,0:T(8,128)(2,1)} %collective-permute-done, ...), kind=kLoop, calls=%fused_computation.8 | loop fusion | flops 40370176 | bytes 29038592 | tf_op jit(solution)/shard_map/add | solution.py:38
  294.9 0.2 slice_bitcast_fusion
  295.1 0.3 fusion.6
  295.4 1.8 fusion.10
  (18 shorter events, 0.1 us)
Async XLA Ops:
  7.2 61.1 %copy-start.3 = (bf16[176]{0:T(256)(128)(2,1)S(1)}, bf16[176]{0:T(256)(128)(2,1)}, u32[]{:S(2)}) copy-start(bf16[176]{0:T(256)(128)(2,1)} %param.9) | copy-start | bytes 1060
  7.2 61.3 %copy-start.4 = (bf16[176]{0:T(256)(128)(2,1)S(1)}, bf16[176]{0:T(256)(128)(2,1)}, u32[]{:S(2)}) copy-start(bf16[176]{0:T(256)(128)(2,1)} %param.11) | copy-start | bytes 1060
  7.2 196.0 %copy-start = (bf16[1,2,64,1120]{3,2,1,0:T(8,128)(2,1)S(1)}, bf16[1,2,64,1120]{3,2,1,0:T(8,128)(2,1)}, u32[]{:S(2)}) copy-start(bf16[1,2,64,1120]{3,2,1,0:T(8,128)(2,1)} %param.7) | copy-start | bytes 860164
  7.2 196.0 %copy-start.1 = (bf16[1,2,64,1120]{3,2,1,0:T(8,128)(2,1)S(1)}, bf16[1,2,64,1120]{3,2,1,0:T(8,128)(2,1)}, u32[]{:S(2)}) copy-start(bf16[1,2,64,1120]{3,2,1,0:T(8,128)(2,1)} %param.6) | copy-start | bytes 860164
  7.2 196.1 %all-gather.4.cloned.1.call-start = ((), (), s32[]{:S(2)}) async-start(), calls=%async_computation | async-start | bytes 13381632 | tf_op jit(solution)/shard_map/all_gather | solution.py:73
  211.9 11.8 %copy-start.2 = (bf16[9,176]{1,0:T(8,128)(2,1)S(1)}, bf16[9,176]{1,0:T(8,128)(2,1)}, u32[]{:S(2)}) copy-start(bf16[9,176]{1,0:T(8,128)(2,1)} %param.10) | copy-start | bytes 9508
  213.7 70.6 %collective-permute-start.1 = (bf16[2,1,1,64,5632]{4,3,2,1,0:T(8,128)(2,1)}, bf16[2,1,1,64,5632]{4,3,2,1,0:T(8,128)(2,1)}, u32[]{:S(2)}, u32[]{:S(2)}) collective-permute-start(bf16[2,1,1,64,5632]{4,3,2,1,0:T(8,128)(2,1)} %get-tuple-element.18), channel_id=1, source_target_pairs={{1,0},{2,1},{3,2},{4,3},{5,4},{6,5},{7,6},{8,7},{9,8},{10,9},{11,1... | collective-permute-start | bytes 4325384 | tf_op jit(solution)/shard_map/ppermute | solution.py:17
  221.8 62.5 %collective-permute-start = (bf16[2,1,1,64,5632]{4,3,2,1,0:T(8,128)(2,1)}, bf16[2,1,1,64,5632]{4,3,2,1,0:T(8,128)(2,1)}, u32[]{:S(2)}, u32[]{:S(2)}) collective-permute-start(bf16[2,1,1,64,5632]{4,3,2,1,0:T(8,128)(2,1)} %get-tuple-element.17), channel_id=1, source_target_pairs={{0,1},{1,2},{2,3},{3,4},{4,5},{5,6},{6,7},{7,8},{8,9},{9,10},{10,1... | collective-permute-start | bytes 4325384 | tf_op jit(solution)/shard_map/ppermute | solution.py:15
Sparse Core Ops, SparseCore 0:
  66.4 89.6 all-gather.3
where the time goes:
time: 304 us
  blocking collectives  252 us (83%)
  other arithmetic  14.9 us (5%)
  between operations  14.9 us (5%)
  starting transfers between devices  10 us (3%)
  matrix products  7.05 us (2%)
  local copies, waits for them, and re-layouts  5.29 us (2%)
    unnamed x1, blocking collectives  134 us
    all_gather x1, blocking collectives, on_device(): lax.all_gather(w_depth, 'band', axis=1, tiled=True)  59.7 us
    all_gather x1, blocking collectives, on_device(): weight_rows = lax.all_gather(w_expand, 'img', axis=0, tiled=True)  57.8 us
    ppermute x1, starting transfers between devices, extended(): lax.ppermute(head, axis, [((i + 1) % count, i) for i in range(ends)])  8.08 us
    dot_general x1, matrix products, on_device(): jnp.dot(stacked, lax.all_gather(weight_rows, 'band', axis=1, tiled=True),...  7.05 us
    add x1, other arithmetic, depthwise(): total + window * depth_taps[3 * row_off + col_off].astype(jnp.float32)  6.78 us
  transfers between devices with their start and end apart: 3, of which 0 were waited for; matrix products, arithmetic and copies ran while one was open for 1% of the time, Pallas kernels for 0%

commit v1 on v0

--- a/solution.py
+++ b/solution.py
@@ -57,7 +57,9 @@
 def on_device(latents, tangents, w_expand, b_expand, w_depth, b_depth):
     image_count, row_count, col_count, channels = latents.shape
     depth_taps, expand_bias, depth_bias = (
-        lax.all_gather(w_depth, "band", axis=1, tiled=True),
+        jnp.concatenate(
+            lax.all_to_all(jnp.stack([w_depth] * lax.axis_size("band")), "band", 0, 0), axis=1
+        ),
         lax.all_gather(b_expand, "band", axis=0, tiled=True),
         lax.all_gather(b_depth, "band", axis=0, tiled=True),
     )

time: 304 us -> 277 us (0.911)
  the two profiles are of different devices: /device:TPU:33 before, /device:TPU:1 now
where the time goes in v1:
time: 277 us
  blocking collectives  199 us (72%)
  waiting for transfers between devices  17.8 us (6%)
  starting transfers between devices  15.3 us (6%)
  other arithmetic  15.2 us (5%)
  between operations  14.9 us (5%)
  local copies, waits for them, and re-layouts  7.26 us (3%)
  matrix products  7.05 us (3%)
    unnamed x1, blocking collectives  140 us
    all_gather x1, blocking collectives, on_device(): weight_rows = lax.all_gather(w_expand, 'img', axis=0, tiled=True)  59.5 us
    all_to_all x1, waiting for transfers between devices, on_device(): lax.all_to_all(jnp.stack([w_depth] * lax.axis_size('band')), 'band', 0, 0)  17.8 us
    ppermute x1, starting transfers between devices, extended(): lax.ppermute(head, axis, [((i + 1) % count, i) for i in range(ends)])  8.18 us
    dot_general x1, matrix products, on_device(): jnp.dot(stacked, lax.all_gather(weight_rows, 'band', axis=1, tiled=True),...  7.05 us
    add x1, other arithmetic, depthwise(): total + window * depth_taps[3 * row_off + col_off].astype(jnp.float32)  6.78 us
  transfers between devices with their start and end apart: 4, of which 1 were waited for; matrix products, arithmetic and copies ran while one was open for 2% of the time, Pallas kernels for 0%

profile of v1, /device:TPU:1, one launch (start us, length us, event | category | flops | bytes accessed | tf_op | source)
XLA Modules:
  0.0 276.6 jit_solution(14233562190022145726)
XLA Ops:
  7.3 59.5 %all-gather = bf16[16,70,176]{2,1,0:T(8,128)(2,1)S(1)} all-gather(bf16[1,70,176]{2,1,0:T(8,128)(2,1)} %bitcast.29), channel_id=1, replica_groups=mesh['img'=16,'band'=32] {'img'}, dimensions={0}, use_global_device_ids=true | all-gather | bytes 418880 | tf_op jit(solution)/shard_map/all_gather | solution.py:72
  66.7 0.2 reshape.167
  67.0 1.0 copy.28
  68.0 1.3 dynamic-slice
  69.9 0.2 dynamic-update-slice
  70.2 0.2 dynamic-update-slice.1
  70.4 139.7 %all-reduce.3 = (bf16[5632]{0:T(1024)(128)(2,1)S(1)}, bf16[5632]{0:T(1024)(128)(2,1)S(1)}) all-reduce(bf16[5632]{0:T(1024)(128)(2,1)S(1)} %dynamic-update-slice, bf16[5632]{0:T(1024)(128)(2,1)S(1)} %dynamic-update-slice.1), channel_id=1, replica_groups=mesh['img'=16,'band'=32] {'band'}, use_global_device_ids=true, to_apply=%add.1 | all-reduce | flops 11264 | bytes 45056
  210.2 7.0 %fusion.22 = f32[256,5632]{1,0:T(8,128)S(1)} fusion(bf16[256,1120]{1,0:T(8,128)(2,1)S(1)} %bitcast.26, bf16[1120,5632]{0,1:T(8,128)(2,1)} %all-gather.3.cloned.1.call-done), kind=kOutput, calls=%fused_computation.48 | convolution fusion | flops 3229614080 | bytes 18956288 | tf_op jit(solution)/shard_map/dot_general | solution.py:73
  217.2 1.4 multiply_convert_fusion
  218.6 0.2 pad_maximum_fusion.2
  218.8 1.8 fusion.21
  220.6 8.2 %collective-permute-start.1 = (bf16[2,1,1,64,5632]{4,3,2,1,0:T(8,128)(2,1)}, bf16[2,1,1,64,5632]{4,3,2,1,0:T(8,128)(2,1)}, u32[]{:S(2)}, u32[]{:S(2)}) collective-permute-start(bf16[2,1,1,64,5632]{4,3,2,1,0:T(8,128)(2,1)} %get-tuple-element.18), channel_id=1, source_target_pairs={{1,0},{2,1},{3,2},{4,3},{5,4},{6,5},{7,6},{8,7},{9,8},{10,9},{11,1... | collective-permute-start | bytes 4325384 | tf_op jit(solution)/shard_map/ppermute | solution.py:17
  228.8 1.9 collective-permute-start
  230.7 1.0 reshape.177
  231.7 5.1 %all-to-all-start = ((bf16[32,2,792]{2,1,0:T(2,128)(2,1)}), bf16[32,2,792]{2,1,0:T(2,128)(2,1)S(1)}, u32[]{:S(2)}, u32[]{:S(2)}) async-start(bf16[32,2,792]{2,1,0:T(2,128)(2,1)} %reshape.177), calls=%async_computation | async-start | bytes 229376 | tf_op jit(solution)/shard_map/all_to_all | solution.py:61
  236.9 17.8 %all-to-all-done = bf16[32,2,792]{2,1,0:T(2,128)(2,1)S(1)} async-done(((bf16[32,2,792]{2,1,0:T(2,128)(2,1)}), bf16[32,2,792]{2,1,0:T(2,128)(2,1)S(1)}, u32[]{:S(2)}, u32[]{:S(2)}) %all-to-all-start) | async-done | bytes 101408 | tf_op jit(solution)/shard_map/all_to_all | solution.py:61
  254.7 0.5 reshape.178
  255.1 0.8 fusion.20
  255.9 0.1 reshape.154
  256.8 3.8 %fusion.5 = bf16[2,1,4,66,5632]{4,3,2,1,0:T(8,128)(2,1)S(1)} fusion(bf16[2,1,1,64,5632]{4,3,2,1,0:T(8,128)(2,1)} %collective-permute-done.1, bf16[2,1,2,64,5632]{4,3,2,1,0:T(8,128)(2,1)S(1)} %bitcast.23, bf16[2,1,1,64,5632]{4,3,2,1,0:T(8,128)(2,1)} %collective-permute-done), kind=kLoop, calls=%fused_computation.7 | loop fusion | flops 35684352 | bytes 11714560 | tf_op jit(solution)/shard_map/concatenate | solution.py:13
  260.6 6.8 %multiply_add_fusion = f32[2,1,2,64,5632]{4,3,2,1,0:T(8,128)S(1)} fusion(bf16[2,1,2,64,5632]{4,3,2,1,0:T(8,128)(2,1)S(1)} %bitcast.24, bf16[2,1,4,66,5632]{4,3,2,1,0:T(8,128)(2,1)S(1)} %fusion.5, bf16[2,1,1,64,5632]{4,3,2,1,0:T(8,128)(2,1)} %collective-permute-done.1, bf16[2,1,1,64,5632]{4,3,2,1,0:T(8,128)(2,1)} %collective-permute-done, ...), kind=kLoop, calls=%fused_computation.8 | loop fusion | flops 40370176 | bytes 29038592 | tf_op jit(solution)/shard_map/add | solution.py:38
  267.4 0.2 slice_bitcast_fusion
  267.6 0.3 fusion.6
  267.9 1.9 fusion.10
  (29 shorter events, 0.9 us)
Async XLA Ops:
  7.2 62.7 %copy-start.3 = (bf16[176]{0:T(256)(128)(2,1)S(1)}, bf16[176]{0:T(256)(128)(2,1)}, u32[]{:S(2)}) copy-start(bf16[176]{0:T(256)(128)(2,1)} %param.9) | copy-start | bytes 1060
  7.2 63.0 %copy-start.4 = (bf16[176]{0:T(256)(128)(2,1)S(1)}, bf16[176]{0:T(256)(128)(2,1)}, u32[]{:S(2)}) copy-start(bf16[176]{0:T(256)(128)(2,1)} %param.11) | copy-start | bytes 1060
  7.2 202.9 %copy-start = (bf16[1,2,64,1120]{3,2,1,0:T(8,128)(2,1)S(1)}, bf16[1,2,64,1120]{3,2,1,0:T(8,128)(2,1)}, u32[]{:S(2)}) copy-start(bf16[1,2,64,1120]{3,2,1,0:T(8,128)(2,1)} %param.7) | copy-start | bytes 860164
  7.2 202.9 %copy-start.1 = (bf16[1,2,64,1120]{3,2,1,0:T(8,128)(2,1)S(1)}, bf16[1,2,64,1120]{3,2,1,0:T(8,128)(2,1)}, u32[]{:S(2)}) copy-start(bf16[1,2,64,1120]{3,2,1,0:T(8,128)(2,1)} %param.6) | copy-start | bytes 860164
  7.2 203.0 %all-gather.3.cloned.1.call-start = ((), (), s32[]{:S(2)}) async-start(), calls=%async_computation.1 | async-start | bytes 13381632 | tf_op jit(solution)/shard_map/all_gather | solution.py:75
  218.8 11.9 %copy-start.2 = (bf16[9,176]{1,0:T(8,128)(2,1)S(1)}, bf16[9,176]{1,0:T(8,128)(2,1)}, u32[]{:S(2)}) copy-start(bf16[9,176]{1,0:T(8,128)(2,1)} %param.10) | copy-start | bytes 9508
  220.6 36.2 %collective-permute-start.1 = (bf16[2,1,1,64,5632]{4,3,2,1,0:T(8,128)(2,1)}, bf16[2,1,1,64,5632]{4,3,2,1,0:T(8,128)(2,1)}, u32[]{:S(2)}, u32[]{:S(2)}) collective-permute-start(bf16[2,1,1,64,5632]{4,3,2,1,0:T(8,128)(2,1)} %get-tuple-element.18), channel_id=1, source_target_pairs={{1,0},{2,1},{3,2},{4,3},{5,4},{6,5},{7,6},{8,7},{9,8},{10,9},{11,1... | collective-permute-start | bytes 4325384 | tf_op jit(solution)/shard_map/ppermute | solution.py:17
  228.8 28.0 %collective-permute-start = (bf16[2,1,1,64,5632]{4,3,2,1,0:T(8,128)(2,1)}, bf16[2,1,1,64,5632]{4,3,2,1,0:T(8,128)(2,1)}, u32[]{:S(2)}, u32[]{:S(2)}) collective-permute-start(bf16[2,1,1,64,5632]{4,3,2,1,0:T(8,128)(2,1)} %get-tuple-element.17), channel_id=1, source_target_pairs={{0,1},{1,2},{2,3},{3,4},{4,5},{5,6},{6,7},{7,8},{8,9},{9,10},{10,1... | collective-permute-start | bytes 4325384 | tf_op jit(solution)/shard_map/ppermute | solution.py:15
  231.7 22.9 %all-to-all-start = ((bf16[32,2,792]{2,1,0:T(2,128)(2,1)}), bf16[32,2,792]{2,1,0:T(2,128)(2,1)S(1)}, u32[]{:S(2)}, u32[]{:S(2)}) async-start(bf16[32,2,792]{2,1,0:T(2,128)(2,1)} %reshape.177), calls=%async_computation | async-start | bytes 229376 | tf_op jit(solution)/shard_map/all_to_all | solution.py:61
Sparse Core Ops, SparseCore 0:
  68.1 89.3 all-gather.2
